TPU v7x, 256 devices: a whole 4x4x8 slice. The times are simulated.
256 devices in a mesh: row: 8 (over z), col: 32 (over x, y, core).
Axes of the slice: x: 4, y: 4, z: 8, core: 2. Of those that a mesh axis runs over, the one named last changes fastest.
Arguments:
- a_trail: float32 [16384, 16384], P('row', 'col'), may hold values from -60 to 60, as said below
- a_panel: float32 [16384, 256], P(('row', 'col')), may hold values from -6 to 6
- l_panel: float32 [16384, 256], P(('row', 'col')), may hold values from -0.5 to 0.5
- a_diag: float32 [256, 256], replicated, may hold values from -60 to 60, as said below
- l_inverse: float32 [256, 256], replicated, may hold values from -4 to 4, as said below
Outputs:
- trail_out: float32 [16384, 16384], P('row', 'col')
- panel_out: float32 [16384, 256], P(('row', 'col'))
Inputs may be any that keep to these rules, and one draw needn't show every extreme that they name: `a_trail`: symmetric. `a_diag`: symmetric. `l_inverse`: lower triangular with a positive diagonal.
All inputs are finite; a program needn't handle non-finite values.
Results may differ from a plain program's by a relative error of at most 0.0003.
Values sent between devices are 32-bit elements; how exact they have to be, the bound alone decides.
No kernel may reach another device: no remote copies, remote signals or barrier semaphores. Data moves between devices by JAX's collectives and lax.ppermute only.
A program may use at most 64 MiB of HBM per device.

v0:
```python
import jax
import jax.numpy as jnp
from jax import lax
from jax.sharding import PartitionSpec as P

NS_STEPS = 8


def from_root(block, axis, owner):
    block = jnp.where(lax.axis_index(axis) == owner, block, jnp.zeros_like(block))
    return lax.psum(block, axis)


def product(left, right):
    return jnp.dot(left, right, precision=lax.Precision.HIGHEST, preferred_element_type=jnp.float32)


def newton_inverse(matrix):
    identity = jnp.eye(matrix.shape[0], dtype=jnp.float32)
    approx = identity
    for repeat in range(NS_STEPS):
        approx = product(approx, 2.0 * identity - product(matrix, approx))
    return approx


def right_solve(factor, values):
    return lax.linalg.triangular_solve(
        factor, values, left_side=False, lower=True, transpose_a=True
    )


def shards(a_trail, a_panel, l_panel, a_diag, l_inverse):
    row_dev, col_dev = a_trail.shape
    block_width = a_diag.shape[0]
    row_index = lax.axis_index("row")
    col_index = lax.axis_index("col")
    owner_row = col_index * col_dev // row_dev
    offset = col_index * col_dev - owner_row * row_dev
    a11_new = product(product(l_inverse, a_diag), l_inverse.T)
    solved = product(a_panel, l_inverse.T)
    half_term = 0.5 * product(l_panel, a11_new)
    first_y = solved - half_term
    panel_out = first_y - half_term
    y_rows, l_rows = (
        lax.all_gather(first_y, "col", axis=0, tiled=True),
        lax.all_gather(l_panel, "col", axis=0, tiled=True),
    )
    stacked = jnp.stack(
        (
            lax.dynamic_slice_in_dim(y_rows, offset, col_dev, 0),
            lax.dynamic_slice_in_dim(l_rows, offset, col_dev, 0),
        )
    )
    received = from_root(stacked, "row", owner_row)
    y_cols = received[0]
    l_cols = received[1]
    updated = a_trail - (product(y_rows, l_cols.T) + product(l_rows, y_cols.T))
    got_panel = from_root(updated[:, :block_width], "col", 0)
    global_rows = row_index * row_dev + lax.iota(jnp.int32, row_dev)
    keep_mask = (global_rows >= block_width)[:, None]
    next_panel = jnp.where(keep_mask, got_panel, 0.0)
    picker = (
        global_rows[:, None] - block_width == lax.iota(jnp.int32, block_width)[None, :]
    ).astype(jnp.float32)
    gram, top_block = lax.psum(
        (product(next_panel.T, next_panel), product(picker.T, next_panel)), "row"
    )
    factor = jnp.linalg.cholesky(gram)
    q_rows = right_solve(factor, next_panel)
    q_top = right_solve(factor, top_block)
    identity = jnp.eye(block_width, dtype=jnp.float32)
    g_inverse = newton_inverse(identity + q_top).T
    refl_rows = q_rows + picker
    refl_cols = from_root(lax.dynamic_slice_in_dim(refl_rows, offset, col_dev, 0), "row", owner_row)
    x_rows = product(lax.psum(product(updated, refl_cols), "col"), g_inverse)
    m_core = product(g_inverse.T, lax.psum(product(refl_rows.T, x_rows), "row"))
    z_rows = x_rows - 0.5 * product(refl_rows, m_core)
    z_cols = from_root(lax.dynamic_slice_in_dim(z_rows, offset, col_dev, 0), "row", owner_row)
    trail_out = updated - (product(z_rows, refl_cols.T) + product(refl_rows, z_cols.T))
    return (trail_out, panel_out)


def solution(mesh):
    return jax.shard_map(
        shards,
        mesh=mesh,
        in_specs=(P("row", "col"), P(("row", "col"), None), P(("row", "col"), None), P(), P()),
        out_specs=(P("row", "col"), P(("row", "col"), None)),
        check_vma=False,
    )
```

profile of v0, /device:TPU:2, one launch (start us, length us, event | category | flops | bytes accessed | tf_op | source)
XLA Modules:
  0.0 843.6 jit_solution(7050816020331745766)
XLA Ops:
  13.7 50.7 %all-gather.3.cloned.1.call-done = f32[2048,256]{1,0:T(8,128)} async-done(((f32[64,256]{1,0:T(8,128)}), f32[2048,256]{1,0:T(8,128)}) %all-gather.3.cloned.1.call-update) | async-done | bytes 2097168 | tf_op jit(solution)/shard_map/all_gather | solution.py:45
  65.5 49.6 %all-gather.5.cloned.1.call-done = f32[2048,256]{1,0:T(8,128)} async-done(((f32[64,256]{1,0:T(8,128)}), f32[2048,256]{1,0:T(8,128)}) %all-gather.5.cloned.1.call-update) | async-done | bytes 2097168 | tf_op jit(solution)/shard_map/all_gather | solution.py:46
  117.3 76.4 %all-reduce.10.cloned.1.call-done = f32[2,512,256]{2,1,0:T(8,128)} async-done(((f32[2,512,256]{2,1,0:T(8,128)}), f32[2,512,256]{2,1,0:T(8,128)}) %all-reduce.10.cloned.1.call-update) | async-done | bytes 1048592 | tf_op jit(solution)/shard_map/psum | solution.py:11
  193.7 4.7 fusion.7
  198.4 4.8 fusion
  207.1 115.2 %all-reduce.12.cloned.1.call-done = f32[2048,256]{1,0:T(8,128)} async-done(((f32[2048,256]{1,0:T(8,128)}), f32[2048,256]{1,0:T(8,128)}) %all-reduce.12.cloned.1.call-update) | async-done | bytes 2097168 | tf_op jit(solution)/shard_map/psum | solution.py:11
  324.2 4.2 fusion.25
  330.6 70.8 %all-reduce.14.cloned.1.call-done = f32[256,256]{0,1:T(8,128)} async-done(((f32[256,256]{0,1:T(8,128)}), f32[256,256]{0,1:T(8,128)}) %all-reduce.14.cloned.1.call-update) | async-done | bytes 262160 | tf_op jit(solution)/shard_map/psum | solution.py:65
  403.5 11.7 %cholesky.50 = f32[128,128]{1,0:T(8,128)S(1)} custom-call(f32[128,128]{1,0:T(8,128)S(1)} %cholesky.118), custom_call_target="Cholesky" | custom-call | tf_op jit(solution)/shard_map/jit(cholesky)/cholesky | solution.py:68
  415.3 9.8 %custom-call.16 = f32[1,128,128]{1,2,0:T(8,128)S(1)} custom-call(f32[1,128,128]{2,1,0:T(8,128)S(1)} %get-tuple-element.25), custom_call_target="InvertDiagBlocksLowerTriangular" | custom-call | tf_op jit(solution)/shard_map/jit(cholesky)/cholesky | solution.py:68
  425.6 11.7 %cholesky.105 = f32[128,128]{1,0:T(8,128)S(1)} custom-call(f32[128,128]{1,0:T(8,128)S(1)} %convolution_subtract_fusion.10), custom_call_target="Cholesky" | custom-call | tf_op jit(solution)/shard_map/jit(cholesky)/cholesky | solution.py:68
  439.3 4.0 while.1
  443.3 19.7 %custom-call.17 = f32[2,128,128]{1,2,0:T(8,128)S(1)} custom-call(f32[2,128,128]{2,1,0:T(8,128)S(1)} %get-tuple-element.9), custom_call_target="InvertDiagBlocksLowerTriangular" | custom-call | tf_op jit(solution)/shard_map/triangular_solve | solution.py:27
  468.5 73.0 %all-reduce.22.cloned.1.call-done = (f32[512,256]{0,1:T(8,128)}, f32[256,256]{1,0:T(8,128)}) async-done(((f32[512,256]{0,1:T(8,128)}, f32[256,256]{1,0:T(8,128)}), (f32[512,256]{0,1:T(8,128)}, f32[256,256]{1,0:T(8,128)})) %all-reduce.22.cloned.1.call-update) | async-done | bytes 786448 | tf_op jit(solution)/shard_map/psum | solution.py:11
  549.3 4.9 fusion.26
  557.6 112.1 %all-reduce.16.cloned.1.call-done = f32[2048,256]{1,0:T(8,128)} async-done(((f32[2048,256]{1,0:T(8,128)}), f32[2048,256]{1,0:T(8,128)}) %all-reduce.16.cloned.1.call-update) | async-done | bytes 2097168 | tf_op jit(solution)/shard_map/psum | solution.py:75
  669.7 3.5 fusion.34
  674.6 2.6 fusion.35
  677.4 2.9 copy.13
  680.3 69.8 %all-reduce.18.cloned.1.call-done = f32[256,256]{1,0:T(8,128)} async-done(((f32[256,256]{1,0:T(8,128)}), f32[256,256]{1,0:T(8,128)}) %all-reduce.18.cloned.1.call-update) | async-done | bytes 262160 | tf_op jit(solution)/shard_map/psum | solution.py:76
  751.5 3.8 fusion.1
  757.4 9.9 %fusion.37 = f32[2048,512]{1,0:T(8,128)} fusion(f32[2048,256]{0,1:T(8,128)} %copy-done.4, f32[512,256]{0,1:T(8,128)S(1)} %copy-done.8), kind=kOutput, calls=%fused_computation.84 | convolution fusion | flops 3221225472 | bytes 6815744 | tf_op jit(solution)/shard_map/dot_general | solution.py:15
  767.4 62.0 %all-reduce.20.cloned.1.call-done = f32[512,256]{0,1:T(8,128)} async-done(((f32[512,256]{0,1:T(8,128)}), f32[512,256]{0,1:T(8,128)}) %all-reduce.20.cloned.1.call-update) | async-done | bytes 524304 | tf_op jit(solution)/shard_map/psum | solution.py:11
  829.4 7.5 add_subtract_fusion
  (94 shorter events, 46.4 us)
Async XLA Ops:
  7.2 1.0 copy-start
  7.2 57.2 %all-gather.3.cloned.1.call-start = ((), (), s32[]{:S(2)}) async-start(), calls=%async_computation | async-start | bytes 2162688 | tf_op jit(solution)/shard_map/all_gather | solution.py:45
  12.9 102.2 %all-gather.5.cloned.1.call-start = ((), (), s32[]{:S(2)}) async-start(), calls=%async_computation.1 | async-start | bytes 2162688 | tf_op jit(solution)/shard_map/all_gather | solution.py:46
  13.6 180.0 %all-reduce.10.cloned.1.call-start = ((), (), s32[]{:S(2)}) async-start(), calls=%async_computation.2 | async-start | bytes 2097152 | tf_op jit(solution)/shard_map/psum | solution.py:11
  65.5 128.2 %copy-start.6 = (f32[2048,256]{1,0:T(8,128)S(1)}, f32[2048,256]{1,0:T(8,128)}, u32[]{:S(2)}) copy-start(f32[2048,256]{1,0:T(8,128)} %all-gather.3.cloned.1.call-done) | copy-start | bytes 6291460
  117.3 205.0 %all-reduce.12.cloned.1.call-start = ((), (), s32[]{:S(2)}) async-start(), calls=%async_computation.3 | async-start | bytes 4194304 | tf_op jit(solution)/shard_map/psum | solution.py:11
  193.7 4.7 copy-start.5
  193.7 4.7 copy-start.7
  203.2 2.0 copy-start.1
  206.8 194.6 %all-reduce.14.cloned.1.call-start = ((), (), s32[]{:S(2)}) async-start(), calls=%async_computation.4 | async-start | bytes 524288 | tf_op jit(solution)/shard_map/psum | solution.py:65
  328.4 213.1 %all-reduce.22.cloned.1.call-start = ((), (), s32[]{:S(2)}) async-start(), calls=%async_computation.8 | async-start | bytes 1572864 | tf_op jit(solution)/shard_map/psum | solution.py:11
  468.2 201.5 %all-reduce.16.cloned.1.call-start = ((), (), s32[]{:S(2)}) async-start(), calls=%async_computation.5 | async-start | bytes 4194304 | tf_op jit(solution)/shard_map/psum | solution.py:75
  546.2 3.1 copy-start.2
  546.6 2.7 copy-start.8
  554.2 196.0 %all-reduce.18.cloned.1.call-start = ((), (), s32[]{:S(2)}) async-start(), calls=%async_computation.6 | async-start | bytes 524288 | tf_op jit(solution)/shard_map/psum | solution.py:76
  673.2 1.3 copy-start.3
  677.2 152.2 %all-reduce.20.cloned.1.call-start = ((), (), s32[]{:S(2)}) async-start(), calls=%async_computation.7 | async-start | bytes 1048576 | tf_op jit(solution)/shard_map/psum | solution.py:11
  755.3 1.3 copy-start.4
Sparse Core Ops, SparseCore 0:
  13.0 51.3 all-gather.2
  66.9 48.1 all-gather.4
  118.0 75.5 all-reduce.9
  206.9 115.3 all-reduce.11
  328.6 72.7 all-reduce.13
  468.3 73.1 all-reduce.21
  554.3 115.3 all-reduce.15
  677.3 72.7 all-reduce.17
  757.6 71.7 all-reduce.19
where the time goes:
time: 851 us; the launch traced here: 844 us
  waiting for transfers between devices  680 us (80%)
  matrix products  68.9 us (8%)
  other arithmetic  61.2 us (7%)
  local copies, waits for them, and re-layouts  15.7 us (2%)
  between operations  15.7 us (2%)
    psum x4, waiting for transfers between devices, from_root(): return lax.psum(block, axis)  327 us
    psum x1, waiting for transfers between devices, shards(): x_rows = product(lax.psum(product(updated, refl_cols), 'col'), g_inverse)  112 us
    psum x1, waiting for transfers between devices, shards(): lax.psum((product(next_panel.T, next_panel), product(picker.T, next_panel...  70.8 us
    psum x1, waiting for transfers between devices, shards(): m_core = product(g_inverse.T, lax.psum(product(refl_rows.T, x_rows), 'row'))  69.8 us
    dot_general x31, matrix products, product(): jnp.dot(left, right, precision=lax.Precision.HIGHEST, preferred_element_t...  61.7 us
    all_gather x1, waiting for transfers between devices, shards(): lax.all_gather(first_y, 'col', axis=0, tiled=True)  50.7 us
    all_gather x1, waiting for transfers between devices, shards(): lax.all_gather(l_panel, 'col', axis=0, tiled=True)  49.6 us
    another operation x6, other arithmetic, shards(): factor = jnp.linalg.cholesky(gram)  34 us
  transfers between devices with their start and end apart: 9, of which 9 were waited for; matrix products, arithmetic and copies ran while one was open for 2% of the time, Pallas kernels for 0%

commit v1 on v0

--- a/solution.py
+++ b/solution.py
@@ -2,6 +2,7 @@
 import jax.numpy as jnp
 from jax import lax
 from jax.sharding import PartitionSpec as P
+from jax.lax import all_to_all, axis_size
 
 NS_STEPS = 8
 
@@ -41,10 +42,12 @@
     half_term = 0.5 * product(l_panel, a11_new)
     first_y = solved - half_term
     panel_out = first_y - half_term
-    y_rows, l_rows = (
-        lax.all_gather(first_y, "col", axis=0, tiled=True),
-        lax.all_gather(l_panel, "col", axis=0, tiled=True),
-    )
+
+    def samples_apply(my_tile, dim_i):
+        current_block = jnp.stack(axis_size("col") * [my_tile])
+        return jnp.concatenate(all_to_all(current_block, "col", 0, 0), dim_i)
+
+    y_rows, l_rows = (samples_apply(first_y, 0), lax.all_gather(l_panel, "col", axis=0, tiled=True))
     stacked = jnp.stack(
         (
             lax.dynamic_slice_in_dim(y_rows, offset, col_dev, 0),

time: 851 us -> 811 us (0.953)
  waiting for transfers between devices: 680 us -> 631 us
    all_gather x1 -> x0, waiting for transfers between devices: 50.7 us -> none  [shards(): lax.all_gather(first_y, 'col', axis=0, tiled=True)]
    all_to_all x0 -> x1, waiting for transfers between devices: none -> 26.9 us  [samples_apply(): return jnp.concatenate(all_to_all(current_block, 'col', 0, 0), dim_i)]
    all_gather x1, waiting for transfers between devices: 49.6 us -> 24.5 us  [shards(): lax.all_gather(l_panel, 'col', axis=0, tiled=True)]
  transfers between devices with their start and end apart: 9 -> 9, of which waited for: 9 -> 9; matrix products, arithmetic and copies ran while one was open for 2% -> 3% of each run, Pallas kernels for 0% -> 0%
where the time goes in v1:
time: 811 us; the launch traced here: 802 us
  waiting for transfers between devices  631 us (78%)
  matrix products  68.9 us (8%)
  other arithmetic  61.2 us (8%)
  between operations  16 us (2%)
  local copies, waits for them, and re-layouts  15.6 us (2%)
  starting transfers between devices  9.01 us (1%)
    psum x4, waiting for transfers between devices, from_root(): return lax.psum(block, axis)  327 us
    psum x1, waiting for transfers between devices, shards(): x_rows = product(lax.psum(product(updated, refl_cols), 'col'), g_inverse)  112 us
    psum x1, waiting for transfers between devices, shards(): lax.psum((product(next_panel.T, next_panel), product(picker.T, next_panel...  70.8 us
    psum x1, waiting for transfers between devices, shards(): m_core = product(g_inverse.T, lax.psum(product(refl_rows.T, x_rows), 'row'))  69.8 us
    dot_general x31, matrix products, product(): jnp.dot(left, right, precision=lax.Precision.HIGHEST, preferred_element_t...  61.7 us
    another operation x6, other arithmetic, shards(): factor = jnp.linalg.cholesky(gram)  34 us
    all_to_all x1, waiting for transfers between devices, samples_apply(): return jnp.concatenate(all_to_all(current_block, 'col', 0, 0), dim_i)  26.9 us
    all_gather x1, waiting for transfers between devices, shards(): lax.all_gather(l_panel, 'col', axis=0, tiled=True)  24.5 us
  transfers between devices with their start and end apart: 9, of which 9 were waited for; matrix products, arithmetic and copies ran while one was open for 3% of the time, Pallas kernels for 0%

profile of v1, /device:TPU:2, one launch (start us, length us, event | category | flops | bytes accessed | tf_op | source)
XLA Modules:
  0.0 802.5 jit_solution(4105660120071482601)
XLA Ops:
  14.4 7.6 all-to-all-start
  22.1 26.9 %all-to-all-done = f32[32,64,256]{2,1,0:T(8,128)S(1)} async-done(((f32[32,64,256]{2,1,0:T(8,128)}), f32[32,64,256]{2,1,0:T(8,128)S(1)}, u32[]{:S(2)}, u32[]{:S(2)}) %all-to-all-start) | async-done | bytes 2097184 | tf_op jit(solution)/shard_map/all_to_all | solution.py:48
  49.0 24.5 %all-gather.2.cloned.1.call-done = f32[2048,256]{1,0:T(8,128)} async-done(((f32[64,256]{1,0:T(8,128)}), f32[2048,256]{1,0:T(8,128)}) %all-gather.2.cloned.1.call-update) | async-done | bytes 2097168 | tf_op jit(solution)/shard_map/all_gather | solution.py:50
  75.7 76.4 %all-reduce.10.cloned.1.call-done = f32[2,512,256]{2,1,0:T(8,128)} async-done(((f32[2,512,256]{2,1,0:T(8,128)}), f32[2,512,256]{2,1,0:T(8,128)}) %all-reduce.10.cloned.1.call-update) | async-done | bytes 1048592 | tf_op jit(solution)/shard_map/psum | solution.py:12
  152.1 4.7 fusion.7
  156.8 4.8 fusion
  165.5 115.1 %all-reduce.12.cloned.1.call-done = f32[2048,256]{1,0:T(8,128)} async-done(((f32[2048,256]{1,0:T(8,128)}), f32[2048,256]{1,0:T(8,128)}) %all-reduce.12.cloned.1.call-update) | async-done | bytes 2097168 | tf_op jit(solution)/shard_map/psum | solution.py:12
  282.6 4.2 fusion.25
  288.9 70.8 %all-reduce.14.cloned.1.call-done = f32[256,256]{0,1:T(8,128)} async-done(((f32[256,256]{0,1:T(8,128)}), f32[256,256]{0,1:T(8,128)}) %all-reduce.14.cloned.1.call-update) | async-done | bytes 262160 | tf_op jit(solution)/shard_map/psum | solution.py:68
  361.8 11.7 %cholesky.50 = f32[128,128]{1,0:T(8,128)S(1)} custom-call(f32[128,128]{1,0:T(8,128)S(1)} %cholesky.118), custom_call_target="Cholesky" | custom-call | tf_op jit(solution)/shard_map/jit(cholesky)/cholesky | solution.py:71
  373.6 9.8 %custom-call.16 = f32[1,128,128]{1,2,0:T(8,128)S(1)} custom-call(f32[1,128,128]{2,1,0:T(8,128)S(1)} %get-tuple-element.25), custom_call_target="InvertDiagBlocksLowerTriangular" | custom-call | tf_op jit(solution)/shard_map/jit(cholesky)/cholesky | solution.py:71
  383.9 11.7 %cholesky.105 = f32[128,128]{1,0:T(8,128)S(1)} custom-call(f32[128,128]{1,0:T(8,128)S(1)} %convolution_subtract_fusion.10), custom_call_target="Cholesky" | custom-call | tf_op jit(solution)/shard_map/jit(cholesky)/cholesky | solution.py:71
  397.7 4.2 while.1
  401.9 19.7 %custom-call.17 = f32[2,128,128]{1,2,0:T(8,128)S(1)} custom-call(f32[2,128,128]{2,1,0:T(8,128)S(1)} %get-tuple-element.9), custom_call_target="InvertDiagBlocksLowerTriangular" | custom-call | tf_op jit(solution)/shard_map/triangular_solve | solution.py:28
  427.0 73.0 %all-reduce.22.cloned.1.call-done = (f32[512,256]{0,1:T(8,128)}, f32[256,256]{1,0:T(8,128)}) async-done(((f32[512,256]{0,1:T(8,128)}, f32[256,256]{1,0:T(8,128)}), (f32[512,256]{0,1:T(8,128)}, f32[256,256]{1,0:T(8,128)})) %all-reduce.22.cloned.1.call-update) | async-done | bytes 786448 | tf_op jit(solution)/shard_map/psum | solution.py:12
  507.8 4.9 fusion.26
  516.1 112.1 %all-reduce.16.cloned.1.call-done = f32[2048,256]{1,0:T(8,128)} async-done(((f32[2048,256]{1,0:T(8,128)}), f32[2048,256]{1,0:T(8,128)}) %all-reduce.16.cloned.1.call-update) | async-done | bytes 2097168 | tf_op jit(solution)/shard_map/psum | solution.py:78
  628.2 3.5 fusion.34
  635.9 2.9 copy.13
  638.8 69.8 %all-reduce.18.cloned.1.call-done = f32[256,256]{1,0:T(8,128)} async-done(((f32[256,256]{1,0:T(8,128)}), f32[256,256]{1,0:T(8,128)}) %all-reduce.18.cloned.1.call-update) | async-done | bytes 262160 | tf_op jit(solution)/shard_map/psum | solution.py:79
  710.0 3.8 fusion.1
  716.0 9.9 %fusion.37 = f32[2048,512]{1,0:T(8,128)} fusion(f32[2048,256]{0,1:T(8,128)} %copy-done.4, f32[512,256]{0,1:T(8,128)S(1)} %copy-done.7), kind=kOutput, calls=%fused_computation.84 | convolution fusion | flops 3221225472 | bytes 6815744 | tf_op jit(solution)/shard_map/dot_general | solution.py:16
  725.9 62.0 %all-reduce.20.cloned.1.call-done = f32[512,256]{0,1:T(8,128)} async-done(((f32[512,256]{0,1:T(8,128)}), f32[512,256]{0,1:T(8,128)}) %all-reduce.20.cloned.1.call-update) | async-done | bytes 524304 | tf_op jit(solution)/shard_map/psum | solution.py:12
  788.0 7.5 add_subtract_fusion
  (92 shorter events, 48.9 us)
Async XLA Ops:
  7.2 1.0 copy-start
  7.2 66.3 %all-gather.2.cloned.1.call-start = ((), (), s32[]{:S(2)}) async-start(), calls=%async_computation.1 | async-start | bytes 2162688 | tf_op jit(solution)/shard_map/all_gather | solution.py:50
  14.4 34.6 %all-to-all-start = ((f32[32,64,256]{2,1,0:T(8,128)}), f32[32,64,256]{2,1,0:T(8,128)S(1)}, u32[]{:S(2)}, u32[]{:S(2)}) async-start(f32[32,64,256]{2,1,0:T(8,128)} %stack.8), calls=%async_computation | async-start | bytes 4194304 | tf_op jit(solution)/shard_map/all_to_all | solution.py:48
  22.0 130.1 %all-reduce.10.cloned.1.call-start = ((), (), s32[]{:S(2)}) async-start(), calls=%async_computation.2 | async-start | bytes 2097152 | tf_op jit(solution)/shard_map/psum | solution.py:12
  75.7 205.0 %all-reduce.12.cloned.1.call-start = ((), (), s32[]{:S(2)}) async-start(), calls=%async_computation.3 | async-start | bytes 4194304 | tf_op jit(solution)/shard_map/psum | solution.py:12
  152.1 4.7 copy-start.5
  152.1 4.7 copy-start.6
  161.6 2.0 copy-start.1
  165.2 194.5 %all-reduce.14.cloned.1.call-start = ((), (), s32[]{:S(2)}) async-start(), calls=%async_computation.4 | async-start | bytes 524288 | tf_op jit(solution)/shard_map/psum | solution.py:68
  286.7 213.3 %all-reduce.22.cloned.1.call-start = ((), (), s32[]{:S(2)}) async-start(), calls=%async_computation.8 | async-start | bytes 1572864 | tf_op jit(solution)/shard_map/psum | solution.py:12
  426.7 201.5 %all-reduce.16.cloned.1.call-start = ((), (), s32[]{:S(2)}) async-start(), calls=%async_computation.5 | async-start | bytes 4194304 | tf_op jit(solution)/shard_map/psum | solution.py:78
  504.7 3.1 copy-start.2
  505.1 2.7 copy-start.7
  512.7 196.0 %all-reduce.18.cloned.1.call-start = ((), (), s32[]{:S(2)}) async-start(), calls=%async_computation.6 | async-start | bytes 524288 | tf_op jit(solution)/shard_map/psum | solution.py:79
  631.7 1.3 copy-start.3
  635.7 152.3 %all-reduce.20.cloned.1.call-start = ((), (), s32[]{:S(2)}) async-start(), calls=%async_computation.7 | async-start | bytes 1048576 | tf_op jit(solution)/shard_map/psum | solution.py:12
  713.8 1.3 copy-start.4
Sparse Core Ops, SparseCore 0:
  10.6 62.9 all-gather.1
  76.4 75.6 all-reduce.9
  165.4 115.2 all-reduce.11
  286.9 72.7 all-reduce.13
  426.8 73.1 all-reduce.21
  512.8 115.3 all-reduce.15
  635.8 72.8 all-reduce.17
  716.1 71.8 all-reduce.19
